TPU v7x, 512 devices: a whole 4x4x16 slice. The times are simulated.
512 devices in a mesh: doc: 16 (over y_lo, x, core), blk: 32 (over y_hi, z).
Axes of the slice: x: 4, y: 4 (y_hi: 2, y_lo: 2; y = y_hi * 2 + y_lo), z: 16, core: 2. Of those that a mesh axis runs over, the one named last changes fastest.
Arguments:
- query_rows: bfloat16 [256, 98304], P('blk', 'doc'), may hold values from -6 to 6
- row_values: bfloat16 [16, 32, 32, 128, 256], P('doc', 'blk'), may hold values from -0.25 to 0.25
- row_slots: int32 [16, 32, 32, 128], P('doc', 'blk'), may hold values from 0 to 49151, as said below
- row_counts: int32 [16, 32, 32], P('doc', 'blk'), may hold values from 16 to 128, as said below
Outputs:
- gram: float32 [256, 65536], P('doc', 'blk')
Inputs may be any that keep to these rules, and one draw needn't show every extreme that they name: row_slots[d, s, o, j] = (s * 192 + e) * 8 + b for a document e of source s's 192 and a feature block b of owner o; the 128 entries of one (d, s, o) are distinct. Slots j >= row_counts[d, s, o] carry no data; for every d some owner receives 128 rows from every source.
All inputs are finite; a program needn't handle non-finite values.
Results may differ from a plain program's by a relative error of at most 0.0003.
Values may be sent and summed in bfloat16 or wider, within the bound.
No kernel may reach another device: no remote copies, remote signals or barrier semaphores. Data moves between devices by JAX's collectives and lax.ppermute only.
A program may use at most 192 MiB of HBM per device.

v0:
```python
import jax
import jax.numpy as jnp
from jax import lax
from jax.sharding import PartitionSpec as P

F = 65536
BW = 256


def per_device(query_rows, row_values, row_slots, row_counts):
    owners = lax.axis_size("blk")
    doc_count = query_rows.shape[1]
    own_width = F // owners
    per_owner = own_width // BW
    places = row_slots.shape[3]
    live_slot = jnp.arange(places, dtype=jnp.int32)[None, None, None, :] < row_counts[:, :, :, None]
    targets = jnp.where(live_slot, row_slots, doc_count * per_owner)
    got_values, got_targets = (
        lax.all_to_all(row_values, "blk", split_axis=2, concat_axis=2, tiled=True),
        lax.all_to_all(targets, "blk", split_axis=2, concat_axis=2, tiled=True),
    )
    flat_values = got_values.reshape(-1, BW)
    flat_targets = got_targets.reshape(-1)
    live_rows = flat_targets < doc_count * per_owner
    doc_of = jnp.where(live_rows, flat_targets // per_owner, doc_count).astype(jnp.int32)
    block_of = flat_targets % per_owner
    block_ids = jnp.arange(per_owner, dtype=jnp.int32)
    gathered = lax.all_gather(query_rows, "blk", axis=0, tiled=True)
    safe_doc = jnp.minimum(doc_of, doc_count - 1)
    picked_queries = jnp.take(gathered, safe_doc, axis=1)

    def block_tile(block):
        keep = (live_rows & (block_of == block))[:, None]
        masked = jnp.where(keep, flat_values, jnp.zeros_like(flat_values))
        return jnp.dot(picked_queries, masked, preferred_element_type=jnp.float32)

    tiles = lax.map(block_tile, block_ids)
    partial_value = tiles.transpose(1, 0, 2).reshape(gathered.shape[0], own_width)
    return lax.psum_scatter(partial_value, "doc", scatter_dimension=0, tiled=True)


def solution(mesh):
    in_specs = (
        P("blk", "doc"),
        P("doc", "blk", None, None, None),
        P("doc", "blk", None, None),
        P("doc", "blk", None),
    )
    out_specs = P("doc", "blk")
    return jax.shard_map(
        per_device, mesh=mesh, in_specs=in_specs, out_specs=out_specs, check_vma=False
    )
```

profile of v0, /device:TPU:32, one launch (start us, length us, event | category | flops | bytes accessed | tf_op | source)
XLA Modules:
  0.0 378.6 jit_solution(15423100263397606264)
XLA Ops:
  6.5 0.8 compare_select_fusion.2
  7.4 31.3 %all_to_all.10 = s32[1,1,32,128]{3,1,0,2:T(1,128)S(1)} all-to-all(s32[1,1,32,128]{3,1,0,2:T(1,128)S(1)} %compare_select_fusion.2), channel_id=1, replica_groups=mesh['doc'=16,'blk'=32] {'blk'}, dimensions={2} | all-to-all | bytes 32768 | tf_op jit(solution)/shard_map/all_to_all | solution.py:20
  38.7 5.9 %all-to-all-start.1 = ((bf16[1,1,32,128,256]{4,3,1,0,2:T(8,128)(2,1)}), bf16[1,1,32,128,256]{4,3,1,0,2:T(8,128)(2,1)}, u32[]{:S(2)}, u32[]{:S(2)}) async-start(bf16[1,1,32,128,256]{4,3,1,0,2:T(8,128)(2,1)} %bitcast.35), calls=%async_computation.1 | async-start | bytes 4194304 | tf_op jit(solution)/shard_map/all_to_all | solution.py:19
  45.5 187.5 %all-gather.2.cloned.1.call-done = bf16[256,6144]{1,0:T(8,128)(2,1)} async-done(((bf16[8,6144]{1,0:T(8,128)(2,1)}), bf16[256,6144]{1,0:T(8,128)(2,1)}) %all-gather.2.cloned.1.call-update) | async-done | bytes 3145744 | tf_op jit(solution)/shard_map/all_gather | solution.py:28
  233.0 3.2 copy.10
  236.2 16.9 %gather_fusion = bf16[4096,256]{1,0:T(8,128)(2,1)} fusion(bf16[256,6144]{0,1:T(8,128)(2,1)S(1)} %copy.10, s32[4096]{0:T(1024)S(1)} %broadcast_clamp_fusion), kind=kCustom, calls=%fused_computation | custom fusion | bytes 4210688 | tf_op jit(solution)/shard_map/jit(_take)/gather | solution.py:30
  253.1 1.9 select_bitcast_fusion
  255.1 2.9 copy.11
  258.0 45.3 %while.10 = (s32[]{:T(128)}, f32[8,256,256]{1,2,0:T(8,128)}, s32[8]{0:T(128)S(1)}, s32[4096]{0:T(1024)S(1)}, pred[4096]{0:T(1024)(128)(4,1)S(1)}, /*index=5*/bf1...) while((s32[]{:T(128)}, f32[8,256,256]{1,2,0:T(8,128)}, s32[8]{0:T(128)S(1)}, s32[4096]{0:T(1024)S(1)}, ...), condition=%wide.region_1.2_spmd, body=%wide.region_0.1_spmd.sunk | while | flops 537927680 | bytes 4485733 | solution.py:37
  258.7 0.7 compare_and_fusion.3
  259.4 4.3 %fusion.21 = f32[8,256,256]{1,2,0:T(8,128)} fusion(f32[8,256,256]{1,2,0:T(8,128)} %get-tuple-element.125, s32[]{:T(128)} %get-tuple-element.124, bf16[256,4096]{1,0:T(8,128)(2,1)} %get-tuple-element.138, bf16[4096,256]{1,0:T(8,128)(2,1)} %get-tuple-element.137, pred[4096]{0:T(1024)(128)(4,1)S(1)} %compare_and_fusion.3), kind=kOutput, calls=%fused_computation.5.clone.1 | convolution fusion | flops 537919488 | bytes 4461056 | tf_op jit(solution)/shard_map/while/body/eval_jaxpr/dot_general | solution.py:35
  264.3 0.7 compare_and_fusion.3
  265.0 4.3 %fusion.21 = f32[8,256,256]{1,2,0:T(8,128)} fusion(f32[8,256,256]{1,2,0:T(8,128)} %get-tuple-element.125, s32[]{:T(128)} %get-tuple-element.124, bf16[256,4096]{1,0:T(8,128)(2,1)} %get-tuple-element.138, bf16[4096,256]{1,0:T(8,128)(2,1)} %get-tuple-element.137, pred[4096]{0:T(1024)(128)(4,1)S(1)} %compare_and_fusion.3), kind=kOutput, calls=%fused_computation.5.clone.1 | convolution fusion | flops 537919488 | bytes 4461056 | tf_op jit(solution)/shard_map/while/body/eval_jaxpr/dot_general | solution.py:35
  270.0 0.7 compare_and_fusion.3
  270.7 4.3 %fusion.21 = f32[8,256,256]{1,2,0:T(8,128)} fusion(f32[8,256,256]{1,2,0:T(8,128)} %get-tuple-element.125, s32[]{:T(128)} %get-tuple-element.124, bf16[256,4096]{1,0:T(8,128)(2,1)} %get-tuple-element.138, bf16[4096,256]{1,0:T(8,128)(2,1)} %get-tuple-element.137, pred[4096]{0:T(1024)(128)(4,1)S(1)} %compare_and_fusion.3), kind=kOutput, calls=%fused_computation.5.clone.1 | convolution fusion | flops 537919488 | bytes 4461056 | tf_op jit(solution)/shard_map/while/body/eval_jaxpr/dot_general | solution.py:35
  275.7 0.7 compare_and_fusion.3
  276.4 4.3 %fusion.21 = f32[8,256,256]{1,2,0:T(8,128)} fusion(f32[8,256,256]{1,2,0:T(8,128)} %get-tuple-element.125, s32[]{:T(128)} %get-tuple-element.124, bf16[256,4096]{1,0:T(8,128)(2,1)} %get-tuple-element.138, bf16[4096,256]{1,0:T(8,128)(2,1)} %get-tuple-element.137, pred[4096]{0:T(1024)(128)(4,1)S(1)} %compare_and_fusion.3), kind=kOutput, calls=%fused_computation.5.clone.1 | convolution fusion | flops 537919488 | bytes 4461056 | tf_op jit(solution)/shard_map/while/body/eval_jaxpr/dot_general | solution.py:35
  281.3 0.7 compare_and_fusion.3
  282.0 4.3 %fusion.21 = f32[8,256,256]{1,2,0:T(8,128)} fusion(f32[8,256,256]{1,2,0:T(8,128)} %get-tuple-element.125, s32[]{:T(128)} %get-tuple-element.124, bf16[256,4096]{1,0:T(8,128)(2,1)} %get-tuple-element.138, bf16[4096,256]{1,0:T(8,128)(2,1)} %get-tuple-element.137, pred[4096]{0:T(1024)(128)(4,1)S(1)} %compare_and_fusion.3), kind=kOutput, calls=%fused_computation.5.clone.1 | convolution fusion | flops 537919488 | bytes 4461056 | tf_op jit(solution)/shard_map/while/body/eval_jaxpr/dot_general | solution.py:35
  287.7 4.3 %fusion.21 = f32[8,256,256]{1,2,0:T(8,128)} fusion(f32[8,256,256]{1,2,0:T(8,128)} %get-tuple-element.125, s32[]{:T(128)} %get-tuple-element.124, bf16[256,4096]{1,0:T(8,128)(2,1)} %get-tuple-element.138, bf16[4096,256]{1,0:T(8,128)(2,1)} %get-tuple-element.137, pred[4096]{0:T(1024)(128)(4,1)S(1)} %compare_and_fusion.3), kind=kOutput, calls=%fused_computation.5.clone.1 | convolution fusion | flops 537919488 | bytes 4461056 | tf_op jit(solution)/shard_map/while/body/eval_jaxpr/dot_general | solution.py:35
  293.3 4.3 %fusion.21 = f32[8,256,256]{1,2,0:T(8,128)} fusion(f32[8,256,256]{1,2,0:T(8,128)} %get-tuple-element.125, s32[]{:T(128)} %get-tuple-element.124, bf16[256,4096]{1,0:T(8,128)(2,1)} %get-tuple-element.138, bf16[4096,256]{1,0:T(8,128)(2,1)} %get-tuple-element.137, pred[4096]{0:T(1024)(128)(4,1)S(1)} %compare_and_fusion.3), kind=kOutput, calls=%fused_computation.5.clone.1 | convolution fusion | flops 537919488 | bytes 4461056 | tf_op jit(solution)/shard_map/while/body/eval_jaxpr/dot_general | solution.py:35
  299.0 4.3 %fusion.21 = f32[8,256,256]{1,2,0:T(8,128)} fusion(f32[8,256,256]{1,2,0:T(8,128)} %get-tuple-element.125, s32[]{:T(128)} %get-tuple-element.124, bf16[256,4096]{1,0:T(8,128)(2,1)} %get-tuple-element.138, bf16[4096,256]{1,0:T(8,128)(2,1)} %get-tuple-element.137, pred[4096]{0:T(1024)(128)(4,1)S(1)} %compare_and_fusion.3), kind=kOutput, calls=%fused_computation.5.clone.1 | convolution fusion | flops 537919488 | bytes 4461056 | tf_op jit(solution)/shard_map/while/body/eval_jaxpr/dot_general | solution.py:35
  303.4 2.9 copy.13
  306.3 65.4 %reduce-scatter.2.cloned.1.call-done = f32[16,2048]{1,0:T(8,128)} async-done(((f32[256,2048]{1,0:T(8,128)}), f32[16,2048]{1,0:T(8,128)}) %reduce-scatter.2.cloned.1.call-update) | async-done | bytes 131088 | tf_op jit(solution)/shard_map/reduce_scatter | solution.py:39
  (22 shorter events, 8.2 us)
Async XLA Ops:
  38.7 219.4 %all-to-all-start.1 = ((bf16[1,1,32,128,256]{4,3,1,0,2:T(8,128)(2,1)}), bf16[1,1,32,128,256]{4,3,1,0,2:T(8,128)(2,1)}, u32[]{:S(2)}, u32[]{:S(2)}) async-start(bf16[1,1,32,128,256]{4,3,1,0,2:T(8,128)(2,1)} %bitcast.35), calls=%async_computation.1 | async-start | bytes 4194304 | tf_op jit(solution)/shard_map/all_to_all | solution.py:19
  44.6 188.5 %all-gather.2.cloned.1.call-start = ((), (), s32[]{:S(2)}) async-start(), calls=%async_computation.3 | async-start | bytes 3244032 | tf_op jit(solution)/shard_map/all_gather | solution.py:28
  45.3 326.5 %reduce-scatter.2.cloned.1.call-start = ((), (), s32[]{:S(2)}) async-start(), calls=%async_computation.4 | async-start | bytes 2228224 | tf_op jit(solution)/shard_map/reduce_scatter | solution.py:39
Sparse Core Ops, SparseCore 0:
  48.5 184.4 all-gather.1
  306.4 65.2 reduce-scatter.1
where the time goes:
time: 379 us
  waiting for transfers between devices  254 us (67%)
  matrix products  34.6 us (9%)
  blocking collectives  31.3 us (8%)
  local copies, waits for them, and re-layouts  31.2 us (8%)
  between operations  13.5 us (4%)
  other arithmetic  8.38 us (2%)
  starting transfers between devices  5.98 us (2%)
    all_gather x1, waiting for transfers between devices, per_device(): gathered = lax.all_gather(query_rows, 'blk', axis=0, tiled=True)  187 us
    reduce_scatter x1, waiting for transfers between devices, per_device(): lax.psum_scatter(partial_value, 'doc', scatter_dimension=0, tiled=True)  65.4 us
    dot_general x8, matrix products, block_tile(): return jnp.dot(picked_queries, masked, preferred_element_type=jnp.float32)  34.6 us
    all_to_all x1, blocking collectives, per_device(): lax.all_to_all(targets, 'blk', split_axis=2, concat_axis=2, tiled=True)  31.3 us
    gather x1, local copies, waits for them, and re-layouts, per_device(): picked_queries = jnp.take(gathered, safe_doc, axis=1)  16.9 us
  transfers between devices with their start and end apart: 3, of which 2 were waited for; matrix products, arithmetic and copies ran while one was open for 7% of the time, Pallas kernels for 0%

commit v1 on v0

--- a/solution.py
+++ b/solution.py
@@ -25,7 +25,9 @@
     doc_of = jnp.where(live_rows, flat_targets // per_owner, doc_count).astype(jnp.int32)
     block_of = flat_targets % per_owner
     block_ids = jnp.arange(per_owner, dtype=jnp.int32)
-    gathered = lax.all_gather(query_rows, "blk", axis=0, tiled=True)
+    gathered = jnp.concatenate(
+        lax.all_to_all(jnp.stack([query_rows] * lax.axis_size("blk")), "blk", 0, 0), axis=0
+    )
     safe_doc = jnp.minimum(doc_of, doc_count - 1)
     picked_queries = jnp.take(gathered, safe_doc, axis=1)
 

time: 379 us -> 411 us (1.084)
  blocking collectives: 31.3 us -> 181 us
  waiting for transfers between devices: 254 us -> 137 us
    all_gather x1 -> x0, waiting for transfers between devices: 187 us -> none  [per_device(): gathered = lax.all_gather(query_rows, 'blk', axis=0, tiled=True)]
    all_to_all x0 -> x1, blocking collectives: none -> 149 us  [per_device(): lax.all_to_all(jnp.stack([query_rows] * lax.axis_size('blk')), 'blk', 0, 0)]
    all_to_all x1, waiting for transfers between devices: 0.01 us -> 75.1 us  [per_device(): lax.all_to_all(row_values, 'blk', split_axis=2, concat_axis=2, tiled=True)]
  transfers between devices with their start and end apart: 3 -> 2, of which waited for: 2 -> 2; matrix products, arithmetic and copies ran while one was open for 7% -> 6% of each run, Pallas kernels for 0% -> 0%
where the time goes in v1:
time: 411 us
  blocking collectives  181 us (44%)
  waiting for transfers between devices  137 us (33%)
  matrix products  34.6 us (8%)
  local copies, waits for them, and re-layouts  32 us (8%)
  between operations  13.5 us (3%)
  other arithmetic  7.94 us (2%)
  starting transfers between devices  4.87 us (1%)
    all_to_all x1, blocking collectives, per_device(): lax.all_to_all(jnp.stack([query_rows] * lax.axis_size('blk')), 'blk', 0, 0)  149 us
    all_to_all x1, waiting for transfers between devices, per_device(): lax.all_to_all(row_values, 'blk', split_axis=2, concat_axis=2, tiled=True)  75.1 us
    reduce_scatter x1, waiting for transfers between devices, per_device(): lax.psum_scatter(partial_value, 'doc', scatter_dimension=0, tiled=True)  61.8 us
    dot_general x8, matrix products, block_tile(): return jnp.dot(picked_queries, masked, preferred_element_type=jnp.float32)  34.6 us
    all_to_all x1, blocking collectives, per_device(): lax.all_to_all(targets, 'blk', split_axis=2, concat_axis=2, tiled=True)  31.3 us
    gather x1, local copies, waits for them, and re-layouts, per_device(): picked_queries = jnp.take(gathered, safe_doc, axis=1)  17 us
  transfers between devices with their start and end apart: 2, of which 2 were waited for; matrix products, arithmetic and copies ran while one was open for 6% of the time, Pallas kernels for 0%

profile of v1, /device:TPU:32, one launch (start us, length us, event | category | flops | bytes accessed | tf_op | source)
XLA Modules:
  0.0 410.6 jit_solution(14481836137014315188)
XLA Ops:
  6.5 0.8 compare_select_fusion.2
  7.4 31.3 %all_to_all.15 = s32[1,1,32,128]{3,1,0,2:T(1,128)S(1)} all-to-all(s32[1,1,32,128]{3,1,0,2:T(1,128)S(1)} %compare_select_fusion.2), channel_id=1, replica_groups=mesh['doc'=16,'blk'=32] {'blk'}, dimensions={2} | all-to-all | bytes 32768 | tf_op jit(solution)/shard_map/all_to_all | solution.py:20
  38.7 1.2 stack.2
  39.9 149.4 %all_to_all.16 = bf16[32,8,6144]{2,1,0:T(8,128)(2,1)} all-to-all(bf16[32,8,6144]{2,1,0:T(8,128)(2,1)S(1)} %stack.2), channel_id=1, replica_groups=mesh['doc'=16,'blk'=32] {'blk'}, dimensions={0} | all-to-all | bytes 6291456 | tf_op jit(solution)/shard_map/all_to_all | solution.py:29
  189.3 4.8 %all-to-all-start.1 = ((bf16[1,1,32,128,256]{4,3,1,0,2:T(8,128)(2,1)}), bf16[1,1,32,128,256]{4,3,1,0,2:T(8,128)(2,1)}, u32[]{:S(2)}, u32[]{:S(2)}) async-start(bf16[1,1,32,128,256]{4,3,1,0,2:T(8,128)(2,1)} %bitcast.6), calls=%async_computation.1 | async-start | bytes 4194304 | tf_op jit(solution)/shard_map/all_to_all | solution.py:19
  194.3 3.2 copy.13
  197.5 17.0 %gather_fusion = bf16[4096,256]{1,0:T(8,128)(2,1)} fusion(bf16[256,6144]{0,1:T(8,128)(2,1)S(1)} %copy.13, s32[4096]{0:T(1024)S(1)} %broadcast_clamp_fusion), kind=kCustom, calls=%fused_computation | custom fusion | bytes 4210688 | tf_op jit(solution)/shard_map/jit(_take)/gather | solution.py:32
  214.5 1.9 select_bitcast_fusion
  216.5 2.9 copy.14
  219.4 75.1 %all-to-all-done.1 = bf16[1,1,32,128,256]{4,3,1,0,2:T(8,128)(2,1)} async-done(((bf16[1,1,32,128,256]{4,3,1,0,2:T(8,128)(2,1)}), bf16[1,1,32,128,256]{4,3,1,0,2:T(8,128)(2,1)}, u32[]{:S(2)}, u32[]{:S(2)}) %all-to-all-start.1) | async-done | bytes 2097184 | tf_op jit(solution)/shard_map/all_to_all | solution.py:19
  294.5 44.5 %while.10 = (s32[]{:T(128)}, f32[8,256,256]{1,2,0:T(8,128)}, s32[8]{0:T(128)S(1)}, s32[4096]{0:T(1024)S(1)}, pred[4096]{0:T(1024)(128)(4,1)S(1)}, /*index=5*/bf1...) while((s32[]{:T(128)}, f32[8,256,256]{1,2,0:T(8,128)}, s32[8]{0:T(128)S(1)}, s32[4096]{0:T(1024)S(1)}, ...), condition=%wide.region_1.2_spmd, body=%wide.region_0.1_spmd.sunk | while | flops 537927680 | bytes 4485733 | solution.py:39
  295.8 4.3 %fusion.21 = f32[8,256,256]{1,2,0:T(8,128)} fusion(f32[8,256,256]{1,2,0:T(8,128)} %get-tuple-element.132, s32[]{:T(128)} %get-tuple-element.131, bf16[256,4096]{1,0:T(8,128)(2,1)} %get-tuple-element.145, bf16[4096,256]{1,0:T(8,128)(2,1)} %get-tuple-element.144, pred[4096]{0:T(1024)(128)(4,1)S(1)} %compare_and_fusion.3), kind=kOutput, calls=%fused_computation.5.clone.1 | convolution fusion | flops 537919488 | bytes 4461056 | tf_op jit(solution)/shard_map/while/body/eval_jaxpr/dot_general | solution.py:37
  300.7 0.6 compare_and_fusion.3
  301.3 4.3 %fusion.21 = f32[8,256,256]{1,2,0:T(8,128)} fusion(f32[8,256,256]{1,2,0:T(8,128)} %get-tuple-element.132, s32[]{:T(128)} %get-tuple-element.131, bf16[256,4096]{1,0:T(8,128)(2,1)} %get-tuple-element.145, bf16[4096,256]{1,0:T(8,128)(2,1)} %get-tuple-element.144, pred[4096]{0:T(1024)(128)(4,1)S(1)} %compare_and_fusion.3), kind=kOutput, calls=%fused_computation.5.clone.1 | convolution fusion | flops 537919488 | bytes 4461056 | tf_op jit(solution)/shard_map/while/body/eval_jaxpr/dot_general | solution.py:37
  306.2 0.6 compare_and_fusion.3
  306.9 4.3 %fusion.21 = f32[8,256,256]{1,2,0:T(8,128)} fusion(f32[8,256,256]{1,2,0:T(8,128)} %get-tuple-element.132, s32[]{:T(128)} %get-tuple-element.131, bf16[256,4096]{1,0:T(8,128)(2,1)} %get-tuple-element.145, bf16[4096,256]{1,0:T(8,128)(2,1)} %get-tuple-element.144, pred[4096]{0:T(1024)(128)(4,1)S(1)} %compare_and_fusion.3), kind=kOutput, calls=%fused_computation.5.clone.1 | convolution fusion | flops 537919488 | bytes 4461056 | tf_op jit(solution)/shard_map/while/body/eval_jaxpr/dot_general | solution.py:37
  312.4 4.3 %fusion.21 = f32[8,256,256]{1,2,0:T(8,128)} fusion(f32[8,256,256]{1,2,0:T(8,128)} %get-tuple-element.132, s32[]{:T(128)} %get-tuple-element.131, bf16[256,4096]{1,0:T(8,128)(2,1)} %get-tuple-element.145, bf16[4096,256]{1,0:T(8,128)(2,1)} %get-tuple-element.144, pred[4096]{0:T(1024)(128)(4,1)S(1)} %compare_and_fusion.3), kind=kOutput, calls=%fused_computation.5.clone.1 | convolution fusion | flops 537919488 | bytes 4461056 | tf_op jit(solution)/shard_map/while/body/eval_jaxpr/dot_general | solution.py:37
  318.0 4.3 %fusion.21 = f32[8,256,256]{1,2,0:T(8,128)} fusion(f32[8,256,256]{1,2,0:T(8,128)} %get-tuple-element.132, s32[]{:T(128)} %get-tuple-element.131, bf16[256,4096]{1,0:T(8,128)(2,1)} %get-tuple-element.145, bf16[4096,256]{1,0:T(8,128)(2,1)} %get-tuple-element.144, pred[4096]{0:T(1024)(128)(4,1)S(1)} %compare_and_fusion.3), kind=kOutput, calls=%fused_computation.5.clone.1 | convolution fusion | flops 537919488 | bytes 4461056 | tf_op jit(solution)/shard_map/while/body/eval_jaxpr/dot_general | solution.py:37
  323.5 4.3 %fusion.21 = f32[8,256,256]{1,2,0:T(8,128)} fusion(f32[8,256,256]{1,2,0:T(8,128)} %get-tuple-element.132, s32[]{:T(128)} %get-tuple-element.131, bf16[256,4096]{1,0:T(8,128)(2,1)} %get-tuple-element.145, bf16[4096,256]{1,0:T(8,128)(2,1)} %get-tuple-element.144, pred[4096]{0:T(1024)(128)(4,1)S(1)} %compare_and_fusion.3), kind=kOutput, calls=%fused_computation.5.clone.1 | convolution fusion | flops 537919488 | bytes 4461056 | tf_op jit(solution)/shard_map/while/body/eval_jaxpr/dot_general | solution.py:37
  328.5 0.6 compare_and_fusion.3
  329.1 4.3 %fusion.21 = f32[8,256,256]{1,2,0:T(8,128)} fusion(f32[8,256,256]{1,2,0:T(8,128)} %get-tuple-element.132, s32[]{:T(128)} %get-tuple-element.131, bf16[256,4096]{1,0:T(8,128)(2,1)} %get-tuple-element.145, bf16[4096,256]{1,0:T(8,128)(2,1)} %get-tuple-element.144, pred[4096]{0:T(1024)(128)(4,1)S(1)} %compare_and_fusion.3), kind=kOutput, calls=%fused_computation.5.clone.1 | convolution fusion | flops 537919488 | bytes 4461056 | tf_op jit(solution)/shard_map/while/body/eval_jaxpr/dot_general | solution.py:37
  334.7 4.3 %fusion.21 = f32[8,256,256]{1,2,0:T(8,128)} fusion(f32[8,256,256]{1,2,0:T(8,128)} %get-tuple-element.132, s32[]{:T(128)} %get-tuple-element.131, bf16[256,4096]{1,0:T(8,128)(2,1)} %get-tuple-element.145, bf16[4096,256]{1,0:T(8,128)(2,1)} %get-tuple-element.144, pred[4096]{0:T(1024)(128)(4,1)S(1)} %compare_and_fusion.3), kind=kOutput, calls=%fused_computation.5.clone.1 | convolution fusion | flops 537919488 | bytes 4461056 | tf_op jit(solution)/shard_map/while/body/eval_jaxpr/dot_general | solution.py:37
  339.0 2.9 copy.16
  341.9 61.8 %reduce-scatter.2.cloned.1.call-done = f32[16,2048]{1,0:T(8,128)} async-done(((f32[256,2048]{1,0:T(8,128)}), f32[16,2048]{1,0:T(8,128)}) %reduce-scatter.2.cloned.1.call-update) | async-done | bytes 131088 | tf_op jit(solution)/shard_map/reduce_scatter | solution.py:41
  (21 shorter events, 8.1 us)
Async XLA Ops:
  189.3 105.3 %all-to-all-start.1 = ((bf16[1,1,32,128,256]{4,3,1,0,2:T(8,128)(2,1)}), bf16[1,1,32,128,256]{4,3,1,0,2:T(8,128)(2,1)}, u32[]{:S(2)}, u32[]{:S(2)}) async-start(bf16[1,1,32,128,256]{4,3,1,0,2:T(8,128)(2,1)} %bitcast.6), calls=%async_computation.1 | async-start | bytes 4194304 | tf_op jit(solution)/shard_map/all_to_all | solution.py:19
  194.1 209.7 %reduce-scatter.2.cloned.1.call-start = ((), (), s32[]{:S(2)}) async-start(), calls=%async_computation.4 | async-start | bytes 2228224 | tf_op jit(solution)/shard_map/reduce_scatter | solution.py:41
Sparse Core Ops, SparseCore 0:
  342.1 61.6 reduce-scatter.1
